TPU v7x, 32 devices: a whole 2x2x4 slice. The times are simulated.
32 devices in a mesh: tile: 4 (over y, x), mom: 2 (over core), ewin: 4 (over z).
Axes of the slice: x: 2, y: 2, z: 4, core: 2. Of those that a mesh axis runs over, the one named last changes fastest.
Arguments:
- green_ret: bfloat16 [2, 4, 4, 512, 1024], P('mom', 'ewin', 'tile'), may hold values from -0.25 to 0.25
- injection: float32 [2, 4, 4, 512], P('mom', 'ewin', 'tile'), may hold values from 0.1 to 1
- mom_shift: int32 [4], replicated, may hold values from 0 to 7, as said below
- phon_off: int32 [8], replicated, may hold values from -4 to 4
- coupling: float32 [4, 8], replicated, may hold values from 0.05 to 1
- tile_nbr: int32 [4, 4], replicated, may hold values from 0 to 3
Outputs:
- sigma_less: bfloat16 [2, 4, 4, 512, 1024], P('mom', 'ewin', None, 'tile')
Inputs may be any that keep to these rules, and one draw needn't show every extreme that they name: `mom_shift`: every residue from 0 to 1 appears among the 4 shifts taken modulo 2.
All inputs are finite; a program needn't handle non-finite values.
Results may differ from a plain program's by a relative error of at most 0.0036.
Values may be sent and summed in bfloat16 or wider, within the bound.
A program may use at most 64 MiB of HBM per device.

v0:
```python
import jax
import jax.numpy as jnp
from jax import lax
from jax.experimental import pallas as pl
from jax.experimental.pallas import tpu as pltpu
from jax.sharding import PartitionSpec as P

HW = 4
NW = 8
LANES = 128
PACK = 16
MESH = pl.DeviceIdType.MESH


def fused_kernel(
    nt, nm, nz, g_ref, gam_ref, shift_ref, off_ref, coup_ref, nbr_ref, out_ref,
    left, stage, cross, diag, held, fin, parts, tab,
    a_send, a_recv, z_send, z_recv, f_send, f_recv, own_sem,
):
    t, m, z = lax.axis_index("tile"), lax.axis_index("mom"), lax.axis_index("ewin")
    orb, width = g_ref.shape
    tall = orb // nt
    qr = tall // nm // 2
    has_up, has_down = z < nz - 1, z > 0

    def dev(tt, mm, zz):
        return {"tile": tt, "mom": mm, "ewin": zz}

    def order(q):
        return q + (q // 2) * (5 - 2 * q)

    ring = order(t)

    def tile_at(i):
        return order(lax.rem(ring + i, nt))

    def mom_at(j):
        return lax.rem(m + j, nm)

    pairs = [(i, j) for i in range(nt) for j in range(nm)]
    barrier = pltpu.get_barrier_semaphore()
    for i, j in pairs[1:]:
        pl.semaphore_signal(barrier, inc=1, device_id=dev(tile_at(i), mom_at(j), z), device_id_type=MESH)

    @pl.when(has_up)
    def _():
        pl.semaphore_signal(barrier, inc=1, device_id=dev(t, m, z + 1), device_id_type=MESH)

    @pl.when(has_down)
    def _():
        pl.semaphore_signal(barrier, inc=1, device_id=dev(t, m, z - 1), device_id_type=MESH)

    def tile_rows(tile):
        return pl.ds(pl.multiple_of(tile * tall, tall), tall)

    def product(slot, tile):
        both = lax.dot_general(
            left[slot], g_ref[tile_rows(tile), :], (((1,), (1,)), ((), ())), preferred_element_type=jnp.float32
        )
        return both[:tall], both[tall:]

    def compute_first(i):
        rows = g_ref[tile_rows(tile_at(i)), :]
        re = rows[:, :orb].astype(jnp.float32) * gam_ref[...]
        im = rows[:, orb:].astype(jnp.float32) * gam_ref[...]
        left[i, :tall, :orb] = re.astype(jnp.bfloat16)
        left[i, :tall, orb:] = im.astype(jnp.bfloat16)
        left[i, tall:, :orb] = im.astype(jnp.bfloat16)
        left[i, tall:, orb:] = (-re).astype(jnp.bfloat16)
        put(i, tile_at(i + 1))

    def triangle():
        return (lax.broadcasted_iota(jnp.int32, (tall, tall), d) for d in (0, 1))

    def put(i, tile):
        re, im = product(i, tile)
        stage[i, :, :, :, :tall] = re.reshape(2, nm, qr, tall).astype(jnp.bfloat16)
        stage[i, :, :, :, tall:] = im.reshape(2, nm, qr, tall).astype(jnp.bfloat16)

    def put_diagonal(i):
        re, im = product(i, tile_at(i))
        row, col = triangle()
        both = jnp.where(row > col, im, re).reshape(nm, 2, qr, tall).astype(jnp.bfloat16)
        diag[i, :, :, :tall] = both[:, 0]
        diag[i, :, :, tall:] = both[:, 1]

    def compute_cross(a):
        re, im = product(lax.rem(a - ring + nt, nt), order(a + 2))
        cross[a, :, :, :tall] = re.reshape(2 * nm, qr, tall).astype(jnp.bfloat16)
        cross[a, :, :, tall:] = im.reshape(2 * nm, qr, tall).astype(jnp.bfloat16)

    def unit_source(u, i, j):
        c = mom_at(j)
        if u == 0:
            return stage.at[i, 0, c]
        if u == 1:
            return stage.at[(i - 1) % nt, 1, c]
        if u == 2:
            q = lax.rem(ring + i, nt)
            return cross.at[lax.rem(q, 2), (q // 2) * nm + c]
        return diag.at[i, c]

    def a_copy(u, i, j, p):
        lo, n = u * qr, qr
        return pltpu.make_async_remote_copy(
            src_ref=unit_source(u, i, j),
            dst_ref=held.at[1, p, j, pl.ds(lo, n)],
            send_sem=a_send.at[u, i, j],
            recv_sem=a_recv.at[u, i, j],
            device_id=dev(tile_at(i), mom_at(j), z),
            device_id_type=MESH,
        )

    def own_copy(u):
        lo, n = u * qr, qr
        return pltpu.make_async_copy(unit_source(u, 0, 0), held.at[1, t, 0, pl.ds(lo, n)], own_sem.at[u])

    def z_copy(u, i, j, up):
        p = tile_at(nt - i)
        lo, n = u * qr, qr
        return pltpu.make_async_remote_copy(
            src_ref=held.at[1, p, j, pl.ds(lo, n)],
            dst_ref=held.at[0 if up else 2, p, j, pl.ds(lo, n)],
            send_sem=z_send.at[0 if up else 1, u, i, j],
            recv_sem=z_recv.at[0 if up else 1, u, i, j],
            device_id=dev(t, m, z + 1 if up else z - 1),
            device_id_type=MESH,
        )

    def send_slot(u, i):
        for j in range(nm):
            if (i, j) == (0, 0):
                own_copy(u).start()
            else:
                a_copy(u, i, j, t).start()

    def forward(u):
        for i, j in pairs:
            if (i, j) == (0, 0):
                own_copy(u).wait()
            else:
                a_copy(u, i, j, tile_at(nt - i)).wait_recv()

            @pl.when(has_up)
            def _():
                z_copy(u, i, j, True).start()

            @pl.when(has_down)
            def _():
                z_copy(u, i, j, False).start()

    for i in range(nt):
        compute_first(i)
        if i == 0:
            pl.semaphore_wait(barrier, nt * nm - 1 + has_up.astype(jnp.int32) + has_down.astype(jnp.int32))
        send_slot(0, i)
    for i in range(nt):
        send_slot(1, i)
    for a in range(2):
        compute_cross(a)
    for i in range(nt):
        send_slot(2, i)
    forward(0)
    for i in range(nt):
        put_diagonal(i)
        send_slot(3, i)
    forward(1)

    @pl.when(jnp.logical_not(has_down))
    def _():
        held[0] = jnp.zeros(held.shape[1:], held.dtype)

    @pl.when(jnp.logical_not(has_up))
    def _():
        held[2] = jnp.zeros(held.shape[1:], held.dtype)

    shifts = [lax.rem(lax.rem(shift_ref[s], nm) + nm, nm) for s in range(shift_ref.shape[0])]
    for diff in range(nm):
        per_off = []
        for o in range(NW):
            acc = jnp.float32(0.0)
            for s in range(len(shifts)):
                acc = acc + jnp.where(shifts[s] == diff, coup_ref[s, o], 0.0)
            per_off.append(acc)
        for d in range(2 * HW + 1):
            acc = jnp.float32(0.0)
            for o in range(NW):
                acc = acc + jnp.where(off_ref[o] + HW == d, per_off[o], 0.0)
            tab[diff, d] = acc

    def part_lo(u, who, mine=True):
        block = (0, 1, ring // 2 if mine else 1 - ring // 2, 0)[u]
        return pl.multiple_of((block * nm + who) * qr, qr)

    def near_copy(u, kk, who):
        lo, n = u * qr, qr
        return pltpu.make_async_remote_copy(
            src_ref=fin.at[kk, :, pl.ds(lo, n)],
            dst_ref=parts.at[u, :, pl.ds(part_lo(u, who), n)],
            send_sem=f_send.at[0, u, kk],
            recv_sem=f_recv.at[0, u, kk],
            device_id=dev(t, mom_at(kk), z),
            device_id_type=MESH,
        )

    def far_copy(u, kk, lo_there):
        lo, n = u * qr, qr
        return pltpu.make_async_remote_copy(
            src_ref=fin.at[kk, :, pl.ds(lo, n)],
            dst_ref=parts.at[(1, 0, 2)[u], :, pl.ds(lo_there, n)],
            send_sem=f_send.at[1, u, kk],
            recv_sem=f_recv.at[1, u, kk],
            device_id=dev(tile_at((1, nt - 1, 2)[u]), mom_at(kk), z),
            device_id_type=MESH,
        )

    def mix(u):
        for i, j in pairs:
            @pl.when(has_down)
            def _():
                z_copy(u, i, j, True).wait_recv()

            @pl.when(has_up)
            def _():
                z_copy(u, i, j, False).wait_recv()

        lo, n = u * qr, qr
        base = part_lo(u, m)
        weight = [[tab[diff, d] for d in range(2 * HW + 1)] for diff in range(nm)]
        wide = 2 * tall // LANES

        @pl.loop(0, n // PACK * wide)
        def _(step):
            r = pl.multiple_of((step // wide) * PACK, PACK)
            rows = pl.ds(pl.multiple_of(lo + r, PACK), PACK)
            cols = pl.ds(pl.multiple_of((step % wide) * LANES, LANES), LANES)
            acc = [[None] * nt for _ in range(nm)]
            for zs in range(3):
                for p in range(nt):
                    src = zs * nt + p
                    for j in range(nm):
                        x = held[zs, p, j, rows, cols].astype(jnp.float32)
                        for kk in range(nm):
                            for e in range(nt):
                                if 0 <= src - e <= 2 * HW:
                                    term = weight[(kk + j) % nm][src - e] * x
                                    acc[kk][e] = term if acc[kk][e] is None else acc[kk][e] + term
            for e in range(nt):
                for kk in range(nm):
                    value = acc[kk][e].astype(jnp.bfloat16)
                    if kk == 0:
                        parts[u, e, pl.ds(pl.multiple_of(base + r, PACK), PACK), cols] = value
                    if kk > 0 or u < 3:
                        fin[kk, e, rows, cols] = value

        for kk in range(nm):
            if u < 3:
                far_copy(u, kk, part_lo(u, m)).start()
            if kk > 0:
                near_copy(u, kk, m).start()

    def landed(u):
        for kk in range(nm):
            who = lax.rem(m + nm - kk, nm)
            if u < 3:
                far_copy(u, kk, part_lo(u, who, False)).wait_recv()
            if kk > 0:
                near_copy(u, kk, who).wait_recv()

    def kept(tile):
        found = jnp.float32(0.0)
        for b in range(nbr_ref.shape[1]):
            found = jnp.where(nbr_ref[t, b] == tile, 1.0, found)
        return found

    def store(part, tile, flip):
        keep = kept(tile)

        @pl.loop(0, nt)
        def _(e):
            re, im = parts[part, e, :, :tall].astype(jnp.float32), parts[part, e, :, tall:].astype(jnp.float32)
            if flip:
                re, im = re.T, -im.T
            re, im = (re * keep).astype(jnp.bfloat16), (im * keep).astype(jnp.bfloat16)
            out_ref[e, :, pl.ds(pl.multiple_of(tile * tall, tall), tall)] = re
            out_ref[e, :, pl.ds(pl.multiple_of(orb + tile * tall, tall), tall)] = im

    def store_diagonal():
        row, col = triangle()
        keep = kept(t)

        @pl.loop(0, nt)
        def _(e):
            packed = [
                parts[3, e, c * qr : (c + 1) * qr, h * tall : (h + 1) * tall] for c in range(nm) for h in range(2)
            ]
            both = jnp.concatenate(packed, axis=0).astype(jnp.float32)
            turned = both.T
            re = jnp.where(row > col, turned, both)
            im = jnp.where(row > col, both, jnp.where(row < col, -turned, 0.0))
            out_ref[e, :, pl.ds(pl.multiple_of(t * tall, tall), tall)] = (re * keep).astype(jnp.bfloat16)
            out_ref[e, :, pl.ds(pl.multiple_of(orb + t * tall, tall), tall)] = (im * keep).astype(jnp.bfloat16)

    forward(2)
    mix(0)
    forward(3)
    mix(1)
    mix(2)
    landed(0)
    landed(1)
    store(0, tile_at(1), False)
    store(1, tile_at(nt - 1), True)
    mix(3)
    landed(2)

    @pl.when(ring < 2)
    def _():
        store(2, tile_at(2), False)

    @pl.when(ring >= 2)
    def _():
        store(2, tile_at(2), True)

    landed(3)
    store_diagonal()

    for u in range(4):
        for kk in range(nm):
            if u < 3:
                far_copy(u, kk, part_lo(u, m)).wait_send()
            if kk > 0:
                near_copy(u, kk, m).wait_send()
        for i, j in pairs:
            if (i, j) != (0, 0):
                a_copy(u, i, j, t).wait_send()

            @pl.when(has_up)
            def _():
                z_copy(u, i, j, True).wait_send()

            @pl.when(has_down)
            def _():
                z_copy(u, i, j, False).wait_send()


def fused(green_ret, injection, mom_shift, phon_off, coupling, tile_nbr):
    nt, nm, nz = lax.axis_size("tile"), lax.axis_size("mom"), lax.axis_size("ewin")
    orbitals, width = green_ret.shape[3:]
    tall = orbitals // nt
    qr = tall // nm // 2
    green = green_ret.reshape(orbitals, width)
    gamma = injection.reshape(1, orbitals)
    vmem, smem = pl.BlockSpec(memory_space=pltpu.VMEM), pl.BlockSpec(memory_space=pltpu.SMEM)
    dma = pltpu.SemaphoreType.DMA
    total = pl.pallas_call(
        lambda *refs: fused_kernel(nt, nm, nz, *refs),
        out_shape=jax.ShapeDtypeStruct((nt, tall, width), jnp.bfloat16),
        in_specs=[vmem, vmem, smem, smem, smem, smem],
        out_specs=vmem,
        scratch_shapes=[
            pltpu.VMEM((nt, 2 * tall, width), jnp.bfloat16),
            pltpu.VMEM((nt, 2, nm, qr, 2 * tall), jnp.bfloat16),
            pltpu.VMEM((2, 2 * nm, qr, 2 * tall), jnp.bfloat16),
            pltpu.VMEM((nt, nm, qr, 2 * tall), jnp.bfloat16),
            pltpu.VMEM((3, nt, nm, 4 * qr, 2 * tall), jnp.bfloat16),
            pltpu.VMEM((nm, nt, 4 * qr, 2 * tall), jnp.bfloat16),
            pltpu.VMEM((4, nt, tall, 2 * tall), jnp.bfloat16),
            pltpu.SMEM((nm, 2 * HW + 1), jnp.float32),
            dma((4, nt, nm)),
            dma((4, nt, nm)),
            dma((2, 4, nt, nm)),
            dma((2, 4, nt, nm)),
            dma((2, 4, nm)),
            dma((2, 4, nm)),
            dma((4,)),
        ],
        compiler_params=pltpu.CompilerParams(collective_id=0, has_side_effects=True),
    )(green, gamma, mom_shift, phon_off, coupling, tile_nbr)
    return total[None, None]


def with_halo(shard, sides, width):
    for axis, dim in sides:
        peers, length = (lax.axis_size(axis), shard.shape[dim])
        up = [(i, (i + 1) % peers) for i in range(peers - 1)]
        down = [(j, i) for i, j in up]
        last = lax.slice_in_dim(shard, length - width, length, axis=dim)
        initial = lax.slice_in_dim(shard, 0, width, axis=dim)
        before = lax.ppermute(last, axis, up)
        after = lax.ppermute(initial, axis, down)
        shard = jnp.concatenate([before, shard, after], axis=dim)
    return shard


def on_device(green_ret, injection, mom_shift, phon_off, coupling, tile_nbr):
    blocks = green_ret[0, 0]
    gamma = injection[0, 0]
    orbitals = blocks.shape[1]
    ntiles = lax.axis_size("tile")
    per_tile = orbitals // ntiles
    real_part = blocks[:, :, :orbitals].astype(jnp.float32)
    imag_part = blocks[:, :, orbitals:].astype(jnp.float32)
    scale = gamma[:, None, :]
    left_re = jnp.concatenate([real_part * scale, imag_part * scale], axis=2).astype(jnp.bfloat16)
    left_im = jnp.concatenate([imag_part * scale, -real_part * scale], axis=2).astype(jnp.bfloat16)
    real_out = jnp.einsum("prk,pck->prc", left_re, blocks, preferred_element_type=jnp.float32)
    imag_out = jnp.einsum("prk,pck->prc", left_im, blocks, preferred_element_type=jnp.float32)
    payload = jnp.concatenate([real_out, imag_out], axis=2).astype(jnp.bfloat16)
    exchanged = lax.all_to_all(payload, "tile", split_axis=1, concat_axis=0, tiled=True)
    energies = exchanged.shape[0]
    rimmed = with_halo(exchanged, (("ewin", 0),), HW)
    extended = lax.all_gather(rimmed[None], "mom", axis=0, tiled=True)
    nmom = lax.axis_size("mom")
    here = lax.axis_index("mom")
    source = jnp.mod(here - mom_shift, nmom)
    onehot = (source[:, None] == jnp.arange(nmom, dtype=jnp.int32)[None, :]).astype(jnp.float32)
    weights = jnp.dot(onehot.T, coupling, precision=lax.Precision.HIGHEST)
    total = jnp.zeros(exchanged.shape, jnp.float32)
    for offset in range(NW):
        start = HW + phon_off[offset]
        piece = lax.dynamic_slice_in_dim(extended, start, energies, 1)
        for moment in range(nmom):
            total = total + weights[moment, offset] * piece[moment].astype(jnp.float32)
    tile_here = lax.axis_index("tile")
    neighbours = lax.dynamic_index_in_dim(tile_nbr, tile_here, 0, keepdims=False)
    coltile = jnp.arange(orbitals, dtype=jnp.int32) // per_tile
    colmask = jnp.any(coltile[:, None] == neighbours[None, :], axis=1).astype(jnp.float32)
    colmask = jnp.concatenate([colmask, colmask])
    result = (total * colmask[None, None, :]).astype(jnp.bfloat16)
    return result[None, None]


def body_for(mesh):
    nt, nm = mesh.shape["tile"], mesh.shape["mom"]

    def body(green_ret, *rest):
        points, orbitals = green_ret.shape[2:4]
        aligned = orbitals % (nt * LANES) == 0 and orbitals % (nt * nm * 2 * PACK) == 0
        if aligned and points == 1 and nt == HW:
            return fused(green_ret, *rest)
        return on_device(green_ret, *rest)

    return body


def solution(mesh):
    placed = (
        P("mom", "ewin", "tile", None, None),
        P("mom", "ewin", "tile", None),
        P(),
        P(),
        P(),
        P(),
    )
    return jax.shard_map(
        body_for(mesh),
        mesh=mesh,
        in_specs=placed,
        out_specs=P("mom", "ewin", None, "tile", None),
        check_vma=False,
    )
```

profile of v0, /device:TPU:0, one launch (start us, length us, event | category | flops | bytes accessed | tf_op | source)
XLA Modules:
  0.0 30.3 jit_solution(1227131597071185509)
XLA Ops:
  0.0 28.0 %shard_map.64 = bf16[4,128,1024]{2,1,0:T(8,128)(2,1)} custom-call(bf16[512,1024]{1,0:T(8,128)(2,1)} %bitcast.4, f32[1,512]{1,0:T(1,128)} %bitcast.5, s32[4]{0:T(128)} %refs_2_.1, s32[8]{0:T(128)} %refs_3_.1, f32[4,8]{1,0:T(4,128)} %refs_4_.1, s32[4,4]{1,0:T(4,128)} %refs_5_.1), custom_call_target="tpu_custom_call" | custom-call | tf_op jit(solution)/shard_map/pallas_call | solution.py:355
  28.0 2.3 %copy.8 = bf16[1,1,4,128,1024]{4,3,2,1,0:T(8,128)(2,1)} copy(bf16[1,1,4,128,1024]{4,3,2,1,0:T(8,128)(2,1)} %bitcast.3) | data formatting | bytes 2097152
where the time goes:
time: 30.5 us; the launch traced here: 30.3 us
  Pallas kernels  28 us (92%)
  local copies, waits for them, and re-layouts  2.26 us (7%)
    pallas_call x1, Pallas kernels, fused(): pl.pallas_call(lambda *refs: fused_kernel(nt, nm, nz, *refs), out_shape=j...  28 us
    unnamed x1, local copies, waits for them, and re-layouts  2.26 us

commit v1 on v0

v1 whole, which is shorter than its diff:
```python
import jax
import jax.numpy as jnp
from jax import lax
from jax.experimental import pallas as pl
from jax.experimental.pallas import tpu as pltpu
from jax.sharding import PartitionSpec as P

HW = 4
NW = 8
LANES = 128
PACK = 16
MESH = pl.DeviceIdType.MESH


def fused_kernel(
    nt, nm, nz, g_ref, gam_ref, shift_ref, off_ref, coup_ref, nbr_ref, out_ref,
    left, stage, held, fin, parts, tab,
    a_send, a_recv, z_send, z_recv, near_send, near_recv, far_send, far_recv, own_sem,
):
    t, m, z = lax.axis_index("tile"), lax.axis_index("mom"), lax.axis_index("ewin")
    orb, width = g_ref.shape
    tall = orb // nt
    qr = tall // nm // 2
    hq = qr // 2
    has_up, has_down = z < nz - 1, z > 0

    def dev(tt, mm, zz):
        return {"tile": tt, "mom": mm, "ewin": zz}

    def order(q):
        return q + (q // 2) * (5 - 2 * q)

    ring = order(t)

    def tile_at(i):
        return order(lax.rem(ring + i, nt))

    def mom_at(j):
        return lax.rem(m + j, nm)

    def share(mm):
        return lax.rem(mm + z, nm)

    mine = share(m)
    up_mom, down_mom = mom_at(nm - 1), mom_at(1 % nm)
    pairs = [(i, j) for i in range(nt) for j in range(nm)]
    barrier = pltpu.get_barrier_semaphore()
    for i, j in pairs[1:]:
        pl.semaphore_signal(barrier, inc=1, device_id=dev(tile_at(i), mom_at(j), z), device_id_type=MESH)

    @pl.when(has_up)
    def _():
        pl.semaphore_signal(barrier, inc=1, device_id=dev(t, up_mom, z + 1), device_id_type=MESH)

    @pl.when(has_down)
    def _():
        pl.semaphore_signal(barrier, inc=1, device_id=dev(t, down_mom, z - 1), device_id_type=MESH)

    def tile_rows(tile):
        return pl.ds(pl.multiple_of(tile * tall, tall), tall)

    def times(slot, right):
        both = lax.dot_general(
            left[slot], right, (((1,), (1,)), ((), ())), preferred_element_type=jnp.float32
        )
        return both[:tall], both[tall:]

    def scale_rows(i):
        rows = g_ref[tile_rows(tile_at(i)), :]
        re = rows[:, :orb].astype(jnp.float32) * gam_ref[...]
        im = rows[:, orb:].astype(jnp.float32) * gam_ref[...]
        left[i, :tall, :orb] = re.astype(jnp.bfloat16)
        left[i, :tall, orb:] = im.astype(jnp.bfloat16)
        left[i, tall:, :orb] = im.astype(jnp.bfloat16)
        left[i, tall:, orb:] = (-re).astype(jnp.bfloat16)

    def triangle():
        return (lax.broadcasted_iota(jnp.int32, (tall, tall), d) for d in (0, 1))

    def put_cross(a):
        first, second = lax.rem(a - ring + nt, nt), lax.rem(a + 2 - ring + nt, nt)
        re, im = times(first, g_ref[tile_rows(order(a + 2)), :])
        re = re.reshape(2, nm, qr, tall).astype(jnp.bfloat16)
        im = im.reshape(2, nm, qr, tall).astype(jnp.bfloat16)
        for h, i in enumerate((first, second)):
            stage[i, :, 0, :, :tall] = re[h]
            stage[i, :, 0, :, tall:] = im[h]

    def put_pair(i):
        here, there = g_ref[tile_rows(tile_at(i)), :], g_ref[tile_rows(tile_at(i + 1)), :]
        re, im = times(i, jnp.concatenate([here, there], axis=0))
        row, col = triangle()
        both = jnp.where(row > col, im[:, :tall], re[:, :tall]).reshape(nm, 2, qr, tall).astype(jnp.bfloat16)
        stage[i, :, 3, :, :tall] = both[:, 0]
        stage[i, :, 3, :, tall:] = both[:, 1]
        for cols, block in ((slice(0, tall), re[:, tall:]), (slice(tall, 2 * tall), im[:, tall:])):
            block = block.reshape(2, nm, 2, hq, tall).astype(jnp.bfloat16)
            for h in range(2):
                for b in range(2):
                    stage[(i + h) % nt, :, 1 + b, h * hq : (h + 1) * hq, cols] = block[h, :, b]

    groups = ((0, 1), (1, 1), (2, 2))
    slots = (0, 1, 3, 2)

    def slot_of(i, j):
        return slots[i] * nm + j

    def a_copy(g, i, j):
        v, n = groups[g]
        to = mom_at(j)
        return pltpu.make_async_remote_copy(
            src_ref=stage.at[i, share(to), pl.ds(v, n)],
            dst_ref=held.at[1, pl.ds(v, n), slot_of(i, j)],
            send_sem=a_send.at[g, i, j],
            recv_sem=a_recv.at[g, i, j],
            device_id=dev(tile_at(i), to, z),
            device_id_type=MESH,
        )

    def own_copy():
        return pltpu.make_async_copy(stage.at[0, mine], held.at[1, pl.ds(0, 4), 0], own_sem)

    def send(g, i):
        for j in range(nm):
            if (i, j) != (0, 0):
                a_copy(g, i, j).start()

    def arrived(g, i):
        for j in range(nm):
            if (i, j) != (0, 0):
                a_copy(g, i, j).wait_recv()

    chunks = (
        (0, 1, 0, 1), (1, 3, 0, 1), (0, 4, 1, nm - 1),
        (0, 1, nm, 2 * nm), (0, 1, 3 * nm, nm),
        (1, 1, nm, 3 * nm), (2, 1, nm, 3 * nm), (3, 1, nm, 3 * nm),
    )
    needs = ((0, 2, 3, 4), (1, 5), (6,), (7,))

    def z_copy(k, up):
        v, n, s, w = chunks[k]
        side = 0 if up else 1
        if s == 0:
            src, dst = stage.at[0, mine, pl.ds(v, n)], held.at[2 * side, pl.ds(v, n), 0]
        else:
            src, dst = held.at[1, pl.ds(v, n), pl.ds(s, w)], held.at[2 * side, pl.ds(v, n), pl.ds(s, w)]
        return pltpu.make_async_remote_copy(
            src_ref=src,
            dst_ref=dst,
            send_sem=z_send.at[side, k],
            recv_sem=z_recv.at[side, k],
            device_id=dev(t, up_mom if up else down_mom, z + 1 if up else z - 1),
            device_id_type=MESH,
        )

    def pass_on(k):
        @pl.when(has_up)
        def _():
            z_copy(k, True).start()

        @pl.when(has_down)
        def _():
            z_copy(k, False).start()

    for i in range(nt):
        scale_rows(i)
    near_a = lax.rem(ring, 2)
    put_cross(near_a)
    pl.semaphore_wait(barrier, nt * nm - 1 + has_up.astype(jnp.int32) + has_down.astype(jnp.int32))
    send(0, 2)
    send(0, 0)
    pass_on(0)
    put_cross(1 - near_a)
    send(0, 1)
    send(0, 3)
    put_pair(0)
    put_pair(3)
    send(1, 0)
    send(2, 0)
    pass_on(1)
    own_copy().start()
    put_pair(1)
    send(1, 1)
    put_pair(2)
    for g, i in ((1, 3), (1, 2), (2, 1), (2, 3), (2, 2)):
        send(g, i)
    for g in range(3):
        arrived(g, 0)
    pass_on(2)

    @pl.when(jnp.logical_not(has_down))
    def _():
        held[0] = jnp.zeros(held.shape[1:], held.dtype)

    @pl.when(jnp.logical_not(has_up))
    def _():
        held[2] = jnp.zeros(held.shape[1:], held.dtype)

    shifts = [lax.rem(lax.rem(shift_ref[s], nm) + nm, nm) for s in range(shift_ref.shape[0])]
    for diff in range(nm):
        per_off = []
        for o in range(NW):
            acc = jnp.float32(0.0)
            for s in range(len(shifts)):
                acc = acc + jnp.where(shifts[s] == diff, coup_ref[s, o], 0.0)
            per_off.append(acc)
        for d in range(2 * HW + 1):
            acc = jnp.float32(0.0)
            for o in range(NW):
                acc = acc + jnp.where(off_ref[o] + HW == d, per_off[o], 0.0)
            tab[diff, d] = acc

    for i in (1, 3):
        arrived(0, i)
    pass_on(3)
    arrived(0, 2)
    pass_on(4)
    for i in (1, 3, 2):
        arrived(1, i)
    pass_on(5)
    for i in (1, 3, 2):
        arrived(2, i)
    pass_on(6)
    pass_on(7)
    own_copy().wait()

    bases = []
    for p in range(nt):
        i = lax.rem(ring - order(p) + nt, nt)
        bases.append((i + (i // 2) * (5 - 2 * i)) * nm)

    def block_lo(block, who):
        return pl.multiple_of((block * nm + share(who)) * qr, qr)

    def pieces(v, who, here):
        if v == 0:
            block = ring // 2 if here else 1 - ring // 2
            return [(0, qr, 2, block_lo(block, who), 2, 2)]
        if v == 3:
            return [(3 * qr, qr, 3, block_lo(0, who), None, None)]
        off = (v - 1) * hq
        return [
            (v * qr + h * hq, hq, h, pl.multiple_of(block_lo(h, who) + off, hq), 1 - h, 1 if h == 0 else nt - 1)
            for h in range(2)
        ]

    def near_copy(v, h, kk, who):
        lo, n, slot, row, _, _ = pieces(v, who, True)[h]
        return pltpu.make_async_remote_copy(
            src_ref=fin.at[kk, :, pl.ds(lo, n)],
            dst_ref=parts.at[slot, :, pl.ds(row, n)],
            send_sem=near_send.at[v, h, kk],
            recv_sem=near_recv.at[v, h, kk],
            device_id=dev(t, mom_at(kk), z),
            device_id_type=MESH,
        )

    def far_copy(v, h, kk, who, here):
        lo, n, _, row, slot, step = pieces(v, who, here)[h]
        return pltpu.make_async_remote_copy(
            src_ref=fin.at[kk, :, pl.ds(lo, n)],
            dst_ref=parts.at[slot, :, pl.ds(row, n)],
            send_sem=far_send.at[v, h, kk],
            recv_sem=far_recv.at[v, h, kk],
            device_id=dev(tile_at(step), mom_at(kk), z),
            device_id_type=MESH,
        )

    def halves(v):
        return range(2 if v in (1, 2) else 1)

    def mix(v):
        for k in needs[v]:
            @pl.when(has_down)
            def _():
                z_copy(k, True).wait_recv()

            @pl.when(has_up)
            def _():
                z_copy(k, False).wait_recv()

        own = pieces(v, m, True)
        weight = [[tab[diff, d] for d in range(2 * HW + 1)] for diff in range(nm)]
        wide = 2 * tall // LANES
        for lo, n, slot, row, _, _ in own:
            @pl.loop(0, n // PACK * wide)
            def _(step):
                r = pl.multiple_of((step // wide) * PACK, PACK)
                inner = pl.ds(pl.multiple_of(lo - v * qr + r, PACK), PACK)
                rows = pl.ds(pl.multiple_of(lo + r, PACK), PACK)
                cols = pl.ds(pl.multiple_of((step % wide) * LANES, LANES), LANES)
                acc = [[None] * nt for _ in range(nm)]
                for zs in range(3):
                    for p in range(nt):
                        src = zs * nt + p
                        for j in range(nm):
                            x = held[zs, v, bases[p] + j, inner, cols].astype(jnp.float32)
                            for kk in range(nm):
                                for e in range(nt):
                                    if 0 <= src - e <= 2 * HW:
                                        term = weight[(kk + j + zs - 1) % nm][src - e] * x
                                        acc[kk][e] = term if acc[kk][e] is None else acc[kk][e] + term
                for e in range(nt):
                    for kk in range(nm):
                        value = acc[kk][e].astype(jnp.bfloat16)
                        if kk == 0:
                            parts[slot, e, pl.ds(pl.multiple_of(row + r, PACK), PACK), cols] = value
                        if kk > 0 or v < 3:
                            fin[kk, e, rows, cols] = value

        for h in halves(v):
            for kk in range(nm):
                if v < 3:
                    far_copy(v, h, kk, m, True).start()
                if kk > 0:
                    near_copy(v, h, kk, m).start()

    def landed(v):
        for h in halves(v):
            for kk in range(nm):
                who = mom_at(nm - kk)
                if v < 3:
                    far_copy(v, h, kk, who, False).wait_recv()
                if kk > 0:
                    near_copy(v, h, kk, who).wait_recv()

    def kept(tile):
        found = jnp.float32(0.0)
        for b in range(nbr_ref.shape[1]):
            found = jnp.where(nbr_ref[t, b] == tile, 1.0, found)
        return found

    def store(part, tile, flip):
        keep = kept(tile)

        @pl.loop(0, nt)
        def _(e):
            re, im = parts[part, e, :, :tall].astype(jnp.float32), parts[part, e, :, tall:].astype(jnp.float32)
            if flip:
                re, im = re.T, -im.T
            re, im = (re * keep).astype(jnp.bfloat16), (im * keep).astype(jnp.bfloat16)
            out_ref[e, :, pl.ds(pl.multiple_of(tile * tall, tall), tall)] = re
            out_ref[e, :, pl.ds(pl.multiple_of(orb + tile * tall, tall), tall)] = im

    def store_diagonal():
        row, col = triangle()
        keep = kept(t)

        @pl.loop(0, nt)
        def _(e):
            packed = [
                parts[3, e, c * qr : (c + 1) * qr, h * tall : (h + 1) * tall] for c in range(nm) for h in range(2)
            ]
            both = jnp.concatenate(packed, axis=0).astype(jnp.float32)
            turned = both.T
            re = jnp.where(row > col, turned, both)
            im = jnp.where(row > col, both, jnp.where(row < col, -turned, 0.0))
            out_ref[e, :, pl.ds(pl.multiple_of(t * tall, tall), tall)] = (re * keep).astype(jnp.bfloat16)
            out_ref[e, :, pl.ds(pl.multiple_of(orb + t * tall, tall), tall)] = (im * keep).astype(jnp.bfloat16)

    for v in range(3):
        mix(v)
    landed(0)

    @pl.when(ring < 2)
    def _():
        store(2, tile_at(2), False)

    @pl.when(ring >= 2)
    def _():
        store(2, tile_at(2), True)

    mix(3)
    landed(1)
    landed(2)
    store(0, tile_at(1), False)
    store(1, tile_at(nt - 1), True)
    landed(3)
    store_diagonal()

    for v in range(4):
        for h in halves(v):
            for kk in range(nm):
                if v < 3:
                    far_copy(v, h, kk, m, True).wait_send()
                if kk > 0:
                    near_copy(v, h, kk, m).wait_send()
    for i, j in pairs[1:]:
        for g in range(3):
            a_copy(g, i, j).wait_send()
    for k in range(len(chunks)):
        @pl.when(has_up)
        def _():
            z_copy(k, True).wait_send()

        @pl.when(has_down)
        def _():
            z_copy(k, False).wait_send()


def fused(green_ret, injection, mom_shift, phon_off, coupling, tile_nbr):
    nt, nm, nz = lax.axis_size("tile"), lax.axis_size("mom"), lax.axis_size("ewin")
    orbitals, width = green_ret.shape[3:]
    tall = orbitals // nt
    qr = tall // nm // 2
    green = green_ret.reshape(orbitals, width)
    gamma = injection.reshape(1, orbitals)
    vmem, smem = pl.BlockSpec(memory_space=pltpu.VMEM), pl.BlockSpec(memory_space=pltpu.SMEM)
    dma = pltpu.SemaphoreType.DMA
    total = pl.pallas_call(
        lambda *refs: fused_kernel(nt, nm, nz, *refs),
        out_shape=pltpu.VMEM((nt, tall, width), jnp.bfloat16),
        in_specs=[vmem, vmem, smem, smem, smem, smem],
        out_specs=vmem,
        scratch_shapes=[
            pltpu.VMEM((nt, 2 * tall, width), jnp.bfloat16),
            pltpu.VMEM((nt, nm, 4, qr, 2 * tall), jnp.bfloat16),
            pltpu.VMEM((3, 4, nt * nm, qr, 2 * tall), jnp.bfloat16),
            pltpu.VMEM((nm, nt, 4 * qr, 2 * tall), jnp.bfloat16),
            pltpu.VMEM((4, nt, tall, 2 * tall), jnp.bfloat16),
            pltpu.SMEM((nm, 2 * HW + 1), jnp.float32),
            dma((3, nt, nm)),
            dma((3, nt, nm)),
            dma((2, 8)),
            dma((2, 8)),
            dma((4, 2, nm)),
            dma((4, 2, nm)),
            dma((4, 2, nm)),
            dma((4, 2, nm)),
            dma,
        ],
        compiler_params=pltpu.CompilerParams(collective_id=0, has_side_effects=True),
    )(green, gamma, mom_shift, phon_off, coupling, tile_nbr)
    return total[None, None]


def with_halo(shard, sides, width):
    for axis, dim in sides:
        peers, length = (lax.axis_size(axis), shard.shape[dim])
        up = [(i, (i + 1) % peers) for i in range(peers - 1)]
        down = [(j, i) for i, j in up]
        last = lax.slice_in_dim(shard, length - width, length, axis=dim)
        initial = lax.slice_in_dim(shard, 0, width, axis=dim)
        before = lax.ppermute(last, axis, up)
        after = lax.ppermute(initial, axis, down)
        shard = jnp.concatenate([before, shard, after], axis=dim)
    return shard


def on_device(green_ret, injection, mom_shift, phon_off, coupling, tile_nbr):
    blocks = green_ret[0, 0]
    gamma = injection[0, 0]
    orbitals = blocks.shape[1]
    ntiles = lax.axis_size("tile")
    per_tile = orbitals // ntiles
    real_part = blocks[:, :, :orbitals].astype(jnp.float32)
    imag_part = blocks[:, :, orbitals:].astype(jnp.float32)
    scale = gamma[:, None, :]
    left_re = jnp.concatenate([real_part * scale, imag_part * scale], axis=2).astype(jnp.bfloat16)
    left_im = jnp.concatenate([imag_part * scale, -real_part * scale], axis=2).astype(jnp.bfloat16)
    real_out = jnp.einsum("prk,pck->prc", left_re, blocks, preferred_element_type=jnp.float32)
    imag_out = jnp.einsum("prk,pck->prc", left_im, blocks, preferred_element_type=jnp.float32)
    payload = jnp.concatenate([real_out, imag_out], axis=2).astype(jnp.bfloat16)
    exchanged = lax.all_to_all(payload, "tile", split_axis=1, concat_axis=0, tiled=True)
    energies = exchanged.shape[0]
    rimmed = with_halo(exchanged, (("ewin", 0),), HW)
    extended = lax.all_gather(rimmed[None], "mom", axis=0, tiled=True)
    nmom = lax.axis_size("mom")
    here = lax.axis_index("mom")
    source = jnp.mod(here - mom_shift, nmom)
    onehot = (source[:, None] == jnp.arange(nmom, dtype=jnp.int32)[None, :]).astype(jnp.float32)
    weights = jnp.dot(onehot.T, coupling, precision=lax.Precision.HIGHEST)
    total = jnp.zeros(exchanged.shape, jnp.float32)
    for offset in range(NW):
        start = HW + phon_off[offset]
        piece = lax.dynamic_slice_in_dim(extended, start, energies, 1)
        for moment in range(nmom):
            total = total + weights[moment, offset] * piece[moment].astype(jnp.float32)
    tile_here = lax.axis_index("tile")
    neighbours = lax.dynamic_index_in_dim(tile_nbr, tile_here, 0, keepdims=False)
    coltile = jnp.arange(orbitals, dtype=jnp.int32) // per_tile
    colmask = jnp.any(coltile[:, None] == neighbours[None, :], axis=1).astype(jnp.float32)
    colmask = jnp.concatenate([colmask, colmask])
    result = (total * colmask[None, None, :]).astype(jnp.bfloat16)
    return result[None, None]


def body_for(mesh):
    nt, nm = mesh.shape["tile"], mesh.shape["mom"]

    def body(green_ret, *rest):
        points, orbitals = green_ret.shape[2:4]
        aligned = orbitals % (nt * LANES) == 0 and orbitals % (nt * nm * 4 * PACK) == 0
        if aligned and points == 1 and nt == HW:
            return fused(green_ret, *rest)
        return on_device(green_ret, *rest)

    return body


def solution(mesh):
    placed = (
        P("mom", "ewin", "tile", None, None),
        P("mom", "ewin", "tile", None),
        P(),
        P(),
        P(),
        P(),
    )
    return jax.shard_map(
        body_for(mesh),
        mesh=mesh,
        in_specs=placed,
        out_specs=P("mom", "ewin", None, "tile", None),
        check_vma=False,
    )
```

time: 30.5 us -> 25.3 us (0.83)
  Pallas kernels: 28 us -> 24.2 us
  local copies, waits for them, and re-layouts: 2.26 us -> 0.97 us
    pallas_call x1, Pallas kernels: 28 us -> 24.2 us  [fused(): pl.pallas_call(lambda *refs: fused_kernel(nt, nm, nz, *refs), out_shape=p...]
    unnamed x1, local copies, waits for them, and re-layouts: 2.26 us -> 0.97 us
where the time goes in v1:
time: 25.3 us; the launch traced here: 25.2 us
  Pallas kernels  24.2 us (96%)
  local copies, waits for them, and re-layouts  0.97 us (4%)
    pallas_call x1, Pallas kernels, fused(): pl.pallas_call(lambda *refs: fused_kernel(nt, nm, nz, *refs), out_shape=p...  24.2 us
    unnamed x1, local copies, waits for them, and re-layouts  0.97 us

profile of v1, /device:TPU:0, one launch (start us, length us, event | category | flops | bytes accessed | tf_op | source)
XLA Modules:
  0.0 25.2 jit_solution(10975948619766723494)
XLA Ops:
  0.0 24.2 %shard_map.64 = bf16[4,128,1024]{2,1,0:T(8,128)(2,1)S(1)} custom-call(bf16[512,1024]{1,0:T(8,128)(2,1)} %bitcast.4, f32[1,512]{1,0:T(1,128)} %bitcast.5, s32[4]{0:T(128)} %refs_2_.1, s32[8]{0:T(128)} %refs_3_.1, f32[4,8]{1,0:T(4,128)} %refs_4_.1, s32[4,4]{1,0:T(4,128)} %refs_5_.1), custom_call_target="tpu_custom_call" | custom-call | tf_op jit(solution)/shard_map/pallas_call | solution.py:410
  24.2 1.0 %copy.8 = bf16[1,1,4,128,1024]{4,3,2,1,0:T(8,128)(2,1)} copy(bf16[1,1,4,128,1024]{4,3,2,1,0:T(8,128)(2,1)S(1)} %bitcast.3) | data formatting | bytes 2097152

commit v2 on v1

--- a/solution.py
+++ b/solution.py
@@ -13,12 +13,12 @@
 
 
 def fused_kernel(
-    nt, nm, nz, g_ref, gam_ref, shift_ref, off_ref, coup_ref, nbr_ref, out_ref,
-    left, stage, held, fin, parts, tab,
-    a_send, a_recv, z_send, z_recv, near_send, near_recv, far_send, far_recv, own_sem,
+    nt, nm, nz, g_hbm, gam_hbm, shift_hbm, off_hbm, coup_hbm, nbr_hbm, out_ref,
+    g_ref, gam_ref, shift_ref, off_ref, coup_ref, nbr_ref, left, stage, held, fin, parts, tab,
+    load_sem, a_send, a_recv, z_send, z_recv, near_send, near_recv, far_send, far_recv, own_sem,
 ):
     t, m, z = lax.axis_index("tile"), lax.axis_index("mom"), lax.axis_index("ewin")
-    orb, width = g_ref.shape
+    orb, width = g_hbm.shape
     tall = orb // nt
     qr = tall // nm // 2
     hq = qr // 2
@@ -34,6 +34,20 @@
 
     def tile_at(i):
         return order(lax.rem(ring + i, nt))
+
+    def tile_rows(tile):
+        return pl.ds(pl.multiple_of(tile * tall, tall), tall)
+
+    def load(i):
+        rows = tile_rows(tile_at(i))
+        return pltpu.make_async_copy(g_hbm.at[rows], g_ref.at[rows], load_sem.at[i])
+
+    loads = [pltpu.make_async_copy(gam_hbm, gam_ref, load_sem.at[nt])]
+    loads += [load(i) for i in (0, 2, 1, 3)]
+    small = ((shift_hbm, shift_ref), (off_hbm, off_ref), (coup_hbm, coup_ref), (nbr_hbm, nbr_ref))
+    small = [pltpu.make_async_copy(src, dst, load_sem.at[nt + 1 + n]) for n, (src, dst) in enumerate(small)]
+    for copy in loads + small:
+        copy.start()
 
     def mom_at(j):
         return lax.rem(m + j, nm)
@@ -55,9 +69,6 @@
     @pl.when(has_down)
     def _():
         pl.semaphore_signal(barrier, inc=1, device_id=dev(t, down_mom, z - 1), device_id_type=MESH)
-
-    def tile_rows(tile):
-        return pl.ds(pl.multiple_of(tile * tall, tall), tall)
 
     def times(slot, right):
         both = lax.dot_general(
@@ -131,11 +142,11 @@
                 a_copy(g, i, j).wait_recv()
 
     chunks = (
-        (0, 1, 0, 1), (1, 3, 0, 1), (0, 4, 1, nm - 1),
-        (0, 1, nm, 2 * nm), (0, 1, 3 * nm, nm),
+        (0, 1, 0, 1), (1, 3, 0, 1), (0, 1, 1, nm - 1),
+        (0, 1, nm, 2 * nm), (0, 1, 3 * nm, nm), (1, 3, 1, nm - 1),
         (1, 1, nm, 3 * nm), (2, 1, nm, 3 * nm), (3, 1, nm, 3 * nm),
     )
-    needs = ((0, 2, 3, 4), (1, 5), (6,), (7,))
+    needs = ((0, 2, 3, 4), (1, 5, 6), (7,), (8,))
 
     def z_copy(k, up):
         v, n, s, w = chunks[k]
@@ -162,6 +173,8 @@
         def _():
             z_copy(k, False).start()
 
+    for copy in loads:
+        copy.wait()
     for i in range(nt):
         scale_rows(i)
     near_a = lax.rem(ring, 2)
@@ -184,9 +197,16 @@
     put_pair(2)
     for g, i in ((1, 3), (1, 2), (2, 1), (2, 3), (2, 2)):
         send(g, i)
-    for g in range(3):
+    arrived(0, 0)
+    pass_on(2)
+    for i in (1, 3):
+        arrived(0, i)
+    pass_on(3)
+    arrived(0, 2)
+    pass_on(4)
+    for g in (1, 2):
         arrived(g, 0)
-    pass_on(2)
+    pass_on(5)
 
     @pl.when(jnp.logical_not(has_down))
     def _():
@@ -196,7 +216,10 @@
     def _():
         held[2] = jnp.zeros(held.shape[1:], held.dtype)
 
+    for copy in small:
+        copy.wait()
     shifts = [lax.rem(lax.rem(shift_ref[s], nm) + nm, nm) for s in range(shift_ref.shape[0])]
+    table = []
     for diff in range(nm):
         per_off = []
         for o in range(NW):
@@ -204,24 +227,20 @@
             for s in range(len(shifts)):
                 acc = acc + jnp.where(shifts[s] == diff, coup_ref[s, o], 0.0)
             per_off.append(acc)
+        row = []
         for d in range(2 * HW + 1):
             acc = jnp.float32(0.0)
             for o in range(NW):
                 acc = acc + jnp.where(off_ref[o] + HW == d, per_off[o], 0.0)
-            tab[diff, d] = acc
-
-    for i in (1, 3):
-        arrived(0, i)
-    pass_on(3)
-    arrived(0, 2)
-    pass_on(4)
+            row.append(acc)
+        table.append(row)
+    for d in range(2 * HW + 1):
+        tab[0, d] = 0.5 * (table[0][d] + table[1][d])
+        tab[1, d] = 0.5 * (table[0][d] - table[1][d])
+
     for i in (1, 3, 2):
         arrived(1, i)
-    pass_on(5)
-    for i in (1, 3, 2):
-        arrived(2, i)
     pass_on(6)
-    pass_on(7)
     own_copy().wait()
 
     bases = []
@@ -280,29 +299,27 @@
                 z_copy(k, False).wait_recv()
 
         own = pieces(v, m, True)
-        weight = [[tab[diff, d] for d in range(2 * HW + 1)] for diff in range(nm)]
+        weight = [[tab[part, d] for d in range(2 * HW + 1)] for part in range(2)]
         wide = 2 * tall // LANES
         for lo, n, slot, row, _, _ in own:
-            @pl.loop(0, n // PACK * wide)
-            def _(step):
-                r = pl.multiple_of((step // wide) * PACK, PACK)
-                inner = pl.ds(pl.multiple_of(lo - v * qr + r, PACK), PACK)
-                rows = pl.ds(pl.multiple_of(lo + r, PACK), PACK)
-                cols = pl.ds(pl.multiple_of((step % wide) * LANES, LANES), LANES)
-                acc = [[None] * nt for _ in range(nm)]
+            for step in range(n // PACK * wide):
+                r = step // wide * PACK
+                inner = pl.ds(lo - v * qr + r, PACK)
+                rows = pl.ds(lo + r, PACK)
+                cols = pl.ds(step % wide * LANES, LANES)
+                acc = [[None] * nt for _ in range(2)]
                 for zs in range(3):
                     for p in range(nt):
                         src = zs * nt + p
-                        for j in range(nm):
-                            x = held[zs, v, bases[p] + j, inner, cols].astype(jnp.float32)
-                            for kk in range(nm):
-                                for e in range(nt):
-                                    if 0 <= src - e <= 2 * HW:
-                                        term = weight[(kk + j + zs - 1) % nm][src - e] * x
-                                        acc[kk][e] = term if acc[kk][e] is None else acc[kk][e] + term
+                        x = [held[zs, v, bases[p] + (j + zs + 1) % 2, inner, cols].astype(jnp.float32) for j in range(2)]
+                        for part, y in enumerate((x[0] + x[1], x[0] - x[1])):
+                            for e in range(nt):
+                                if 0 <= src - e <= 2 * HW:
+                                    term = weight[part][src - e] * y
+                                    acc[part][e] = term if acc[part][e] is None else acc[part][e] + term
                 for e in range(nt):
-                    for kk in range(nm):
-                        value = acc[kk][e].astype(jnp.bfloat16)
+                    for kk, value in enumerate((acc[0][e] + acc[1][e], acc[0][e] - acc[1][e])):
+                        value = value.astype(jnp.bfloat16)
                         if kk == 0:
                             parts[slot, e, pl.ds(pl.multiple_of(row + r, PACK), PACK), cols] = value
                         if kk > 0 or v < 3:
@@ -333,8 +350,7 @@
     def store(part, tile, flip):
         keep = kept(tile)
 
-        @pl.loop(0, nt)
-        def _(e):
+        for e in range(nt):
             re, im = parts[part, e, :, :tall].astype(jnp.float32), parts[part, e, :, tall:].astype(jnp.float32)
             if flip:
                 re, im = re.T, -im.T
@@ -346,8 +362,7 @@
         row, col = triangle()
         keep = kept(t)
 
-        @pl.loop(0, nt)
-        def _(e):
+        for e in range(nt):
             packed = [
                 parts[3, e, c * qr : (c + 1) * qr, h * tall : (h + 1) * tall] for c in range(nm) for h in range(2)
             ]
@@ -358,8 +373,13 @@
             out_ref[e, :, pl.ds(pl.multiple_of(t * tall, tall), tall)] = (re * keep).astype(jnp.bfloat16)
             out_ref[e, :, pl.ds(pl.multiple_of(orb + t * tall, tall), tall)] = (im * keep).astype(jnp.bfloat16)
 
-    for v in range(3):
-        mix(v)
+    mix(0)
+    for i in (1, 3, 2):
+        arrived(2, i)
+    pass_on(7)
+    pass_on(8)
+    mix(1)
+    mix(2)
     landed(0)
 
     @pl.when(ring < 2)
@@ -405,24 +425,29 @@
     qr = tall // nm // 2
     green = green_ret.reshape(orbitals, width)
     gamma = injection.reshape(1, orbitals)
-    vmem, smem = pl.BlockSpec(memory_space=pltpu.VMEM), pl.BlockSpec(memory_space=pltpu.SMEM)
+    vmem, anywhere = pl.BlockSpec(memory_space=pltpu.VMEM), pl.BlockSpec(memory_space=pl.ANY)
+    args = (green, gamma, mom_shift, phon_off, coupling, tile_nbr)
     dma = pltpu.SemaphoreType.DMA
     total = pl.pallas_call(
         lambda *refs: fused_kernel(nt, nm, nz, *refs),
         out_shape=pltpu.VMEM((nt, tall, width), jnp.bfloat16),
-        in_specs=[vmem, vmem, smem, smem, smem, smem],
+        in_specs=[anywhere] * len(args),
         out_specs=vmem,
         scratch_shapes=[
+            pltpu.VMEM(green.shape, green.dtype),
+            pltpu.VMEM(gamma.shape, gamma.dtype),
+            *[pltpu.SMEM(a.shape, a.dtype) for a in args[2:]],
             pltpu.VMEM((nt, 2 * tall, width), jnp.bfloat16),
             pltpu.VMEM((nt, nm, 4, qr, 2 * tall), jnp.bfloat16),
             pltpu.VMEM((3, 4, nt * nm, qr, 2 * tall), jnp.bfloat16),
             pltpu.VMEM((nm, nt, 4 * qr, 2 * tall), jnp.bfloat16),
             pltpu.VMEM((4, nt, tall, 2 * tall), jnp.bfloat16),
             pltpu.SMEM((nm, 2 * HW + 1), jnp.float32),
+            dma((nt + 5,)),
             dma((3, nt, nm)),
             dma((3, nt, nm)),
-            dma((2, 8)),
-            dma((2, 8)),
+            dma((2, 9)),
+            dma((2, 9)),
             dma((4, 2, nm)),
             dma((4, 2, nm)),
             dma((4, 2, nm)),
@@ -430,7 +455,7 @@
             dma,
         ],
         compiler_params=pltpu.CompilerParams(collective_id=0, has_side_effects=True),
-    )(green, gamma, mom_shift, phon_off, coupling, tile_nbr)
+    )(*args)
     return total[None, None]
 
 
@@ -491,7 +516,7 @@
     def body(green_ret, *rest):
         points, orbitals = green_ret.shape[2:4]
         aligned = orbitals % (nt * LANES) == 0 and orbitals % (nt * nm * 4 * PACK) == 0
-        if aligned and points == 1 and nt == HW:
+        if aligned and points == 1 and nt == HW and nm == 2:
             return fused(green_ret, *rest)
         return on_device(green_ret, *rest)
 

time: 25.3 us -> 23.8 us (0.941)
  Pallas kernels: 24.2 us -> 22.6 us
    pallas_call x1, Pallas kernels: 24.2 us -> 22.6 us  [fused(): pl.pallas_call(lambda *refs: fused_kernel(nt, nm, nz, *refs), out_shape=p...]
where the time goes in v2:
time: 23.8 us; the launch traced here: 23.6 us
  Pallas kernels  22.6 us (95%)
  local copies, waits for them, and re-layouts  0.97 us (4%)
    pallas_call x1, Pallas kernels, fused(): pl.pallas_call(lambda *refs: fused_kernel(nt, nm, nz, *refs), out_shape=p...  22.6 us
    unnamed x1, local copies, waits for them, and re-layouts  0.97 us

profile of v2, /device:TPU:0, one launch (start us, length us, event | category | flops | bytes accessed | tf_op | source)
XLA Modules:
  0.0 23.6 jit_solution(9539076309326277110)
XLA Ops:
  0.0 22.6 %shard_map.64 = bf16[4,128,1024]{2,1,0:T(8,128)(2,1)S(1)} custom-call(bf16[512,1024]{1,0:T(8,128)(2,1)} %bitcast.4, f32[1,512]{1,0:T(1,128)} %bitcast.5, s32[4]{0:T(128)} %refs_2_.1, s32[8]{0:T(128)} %refs_3_.1, f32[4,8]{1,0:T(4,128)} %refs_4_.1, s32[4,4]{1,0:T(4,128)} %refs_5_.1), custom_call_target="tpu_custom_call" | custom-call | tf_op jit(solution)/shard_map/pallas_call | solution.py:431
  22.6 1.0 %copy.8 = bf16[1,1,4,128,1024]{4,3,2,1,0:T(8,128)(2,1)} copy(bf16[1,1,4,128,1024]{4,3,2,1,0:T(8,128)(2,1)S(1)} %bitcast.3) | data formatting | bytes 2097152

commit v3 on v2

--- a/solution.py
+++ b/solution.py
@@ -42,33 +42,33 @@
         rows = tile_rows(tile_at(i))
         return pltpu.make_async_copy(g_hbm.at[rows], g_ref.at[rows], load_sem.at[i])
 
+    def mom_at(j):
+        return lax.rem(m + j, nm)
+
+    def share(mm):
+        return lax.rem(mm + z, nm)
+
+    mine = share(m)
+    up_mom, down_mom = mom_at(nm - 1), mom_at(1 % nm)
+    pairs = [(i, j) for i in range(nt) for j in range(nm)]
+    barrier = pltpu.get_barrier_semaphore()
+    for i, j in sorted(pairs[1:], key=lambda pair: pair[0] != nt // 2):
+        pl.semaphore_signal(barrier, inc=1, device_id=dev(tile_at(i), mom_at(j), z), device_id_type=MESH)
+
+    @pl.when(has_up)
+    def _():
+        pl.semaphore_signal(barrier, inc=1, device_id=dev(t, up_mom, z + 1), device_id_type=MESH)
+
+    @pl.when(has_down)
+    def _():
+        pl.semaphore_signal(barrier, inc=1, device_id=dev(t, down_mom, z - 1), device_id_type=MESH)
+
     loads = [pltpu.make_async_copy(gam_hbm, gam_ref, load_sem.at[nt])]
     loads += [load(i) for i in (0, 2, 1, 3)]
     small = ((shift_hbm, shift_ref), (off_hbm, off_ref), (coup_hbm, coup_ref), (nbr_hbm, nbr_ref))
     small = [pltpu.make_async_copy(src, dst, load_sem.at[nt + 1 + n]) for n, (src, dst) in enumerate(small)]
     for copy in loads + small:
         copy.start()
-
-    def mom_at(j):
-        return lax.rem(m + j, nm)
-
-    def share(mm):
-        return lax.rem(mm + z, nm)
-
-    mine = share(m)
-    up_mom, down_mom = mom_at(nm - 1), mom_at(1 % nm)
-    pairs = [(i, j) for i in range(nt) for j in range(nm)]
-    barrier = pltpu.get_barrier_semaphore()
-    for i, j in pairs[1:]:
-        pl.semaphore_signal(barrier, inc=1, device_id=dev(tile_at(i), mom_at(j), z), device_id_type=MESH)
-
-    @pl.when(has_up)
-    def _():
-        pl.semaphore_signal(barrier, inc=1, device_id=dev(t, up_mom, z + 1), device_id_type=MESH)
-
-    @pl.when(has_down)
-    def _():
-        pl.semaphore_signal(barrier, inc=1, device_id=dev(t, down_mom, z - 1), device_id_type=MESH)
 
     def times(slot, right):
         both = lax.dot_general(
@@ -110,7 +110,7 @@
                 for b in range(2):
                     stage[(i + h) % nt, :, 1 + b, h * hq : (h + 1) * hq, cols] = block[h, :, b]
 
-    groups = ((0, 1), (1, 1), (2, 2))
+    groups = ((0, 1), (1, 1), (2, 1), (3, 1))
     slots = (0, 1, 3, 2)
 
     def slot_of(i, j):
@@ -142,11 +142,11 @@
                 a_copy(g, i, j).wait_recv()
 
     chunks = (
-        (0, 1, 0, 1), (1, 3, 0, 1), (0, 1, 1, nm - 1),
-        (0, 1, nm, 2 * nm), (0, 1, 3 * nm, nm), (1, 3, 1, nm - 1),
+        (0, 1, 0, 1), (1, 3, 0, 1), (0, 4, 1, nm - 1),
+        (0, 1, nm, 2 * nm), (0, 1, 3 * nm, nm),
         (1, 1, nm, 3 * nm), (2, 1, nm, 3 * nm), (3, 1, nm, 3 * nm),
     )
-    needs = ((0, 2, 3, 4), (1, 5, 6), (7,), (8,))
+    needs = ((0, 2, 3, 4), (1, 5), (6,), (7,))
 
     def z_copy(k, up):
         v, n, s, w = chunks[k]
@@ -173,40 +173,43 @@
         def _():
             z_copy(k, False).start()
 
-    for copy in loads:
+    base = lax.rem(ring, 2)
+    near, far = lax.rem(base - ring + nt, nt), lax.rem(1 - base - ring + nt, nt)
+    for copy in loads[:3]:
         copy.wait()
-    for i in range(nt):
-        scale_rows(i)
-    near_a = lax.rem(ring, 2)
-    put_cross(near_a)
+    scale_rows(near)
+    put_cross(base)
+    for copy in loads[3:]:
+        copy.wait()
+    scale_rows(far)
+    put_cross(1 - base)
     pl.semaphore_wait(barrier, nt * nm - 1 + has_up.astype(jnp.int32) + has_down.astype(jnp.int32))
     send(0, 2)
     send(0, 0)
     pass_on(0)
-    put_cross(1 - near_a)
     send(0, 1)
     send(0, 3)
+    scale_rows(lax.rem(near + 2, nt))
+    scale_rows(lax.rem(far + 2, nt))
     put_pair(0)
     put_pair(3)
-    send(1, 0)
-    send(2, 0)
+    for g in (1, 2, 3):
+        send(g, 0)
     pass_on(1)
     own_copy().start()
     put_pair(1)
     send(1, 1)
     put_pair(2)
-    for g, i in ((1, 3), (1, 2), (2, 1), (2, 3), (2, 2)):
+    for g, i in ((1, 2), (1, 3), (2, 2), (2, 1), (2, 3), (3, 2), (3, 1), (3, 3)):
         send(g, i)
-    arrived(0, 0)
+    for g in range(4):
+        arrived(g, 0)
     pass_on(2)
     for i in (1, 3):
         arrived(0, i)
     pass_on(3)
     arrived(0, 2)
     pass_on(4)
-    for g in (1, 2):
-        arrived(g, 0)
-    pass_on(5)
 
     @pl.when(jnp.logical_not(has_down))
     def _():
@@ -240,7 +243,7 @@
 
     for i in (1, 3, 2):
         arrived(1, i)
-    pass_on(6)
+    pass_on(5)
     own_copy().wait()
 
     bases = []
@@ -373,13 +376,16 @@
             out_ref[e, :, pl.ds(pl.multiple_of(t * tall, tall), tall)] = (re * keep).astype(jnp.bfloat16)
             out_ref[e, :, pl.ds(pl.multiple_of(orb + t * tall, tall), tall)] = (im * keep).astype(jnp.bfloat16)
 
+    for i in (1, 3, 2):
+        arrived(2, i)
+    pass_on(6)
     mix(0)
     for i in (1, 3, 2):
-        arrived(2, i)
+        arrived(3, i)
     pass_on(7)
-    pass_on(8)
     mix(1)
     mix(2)
+    mix(3)
     landed(0)
 
     @pl.when(ring < 2)
@@ -390,7 +396,6 @@
     def _():
         store(2, tile_at(2), True)
 
-    mix(3)
     landed(1)
     landed(2)
     store(0, tile_at(1), False)
@@ -406,7 +411,7 @@
                 if kk > 0:
                     near_copy(v, h, kk, m).wait_send()
     for i, j in pairs[1:]:
-        for g in range(3):
+        for g in range(4):
             a_copy(g, i, j).wait_send()
     for k in range(len(chunks)):
         @pl.when(has_up)
@@ -444,10 +449,10 @@
             pltpu.VMEM((4, nt, tall, 2 * tall), jnp.bfloat16),
             pltpu.SMEM((nm, 2 * HW + 1), jnp.float32),
             dma((nt + 5,)),
-            dma((3, nt, nm)),
-            dma((3, nt, nm)),
-            dma((2, 9)),
-            dma((2, 9)),
+            dma((4, nt, nm)),
+            dma((4, nt, nm)),
+            dma((2, 8)),
+            dma((2, 8)),
             dma((4, 2, nm)),
             dma((4, 2, nm)),
             dma((4, 2, nm)),

time: 23.8 us -> 23.7 us (level)
  no operation moved by 1% of the time
where the time goes in v3:
time: 23.7 us; the launch traced here: 23.5 us
  Pallas kernels  22.6 us (95%)
  local copies, waits for them, and re-layouts  0.97 us (4%)
    pallas_call x1, Pallas kernels, fused(): pl.pallas_call(lambda *refs: fused_kernel(nt, nm, nz, *refs), out_shape=p...  22.6 us
    unnamed x1, local copies, waits for them, and re-layouts  0.97 us

profile of v3, /device:TPU:0, one launch (start us, length us, event | category | flops | bytes accessed | tf_op | source)
XLA Modules:
  0.0 23.5 jit_solution(7474892988809891284)
XLA Ops:
  0.0 22.6 %shard_map.64 = bf16[4,128,1024]{2,1,0:T(8,128)(2,1)S(1)} custom-call(bf16[512,1024]{1,0:T(8,128)(2,1)} %bitcast.4, f32[1,512]{1,0:T(1,128)} %bitcast.5, s32[4]{0:T(128)} %refs_2_.1, s32[8]{0:T(128)} %refs_3_.1, f32[4,8]{1,0:T(4,128)} %refs_4_.1, s32[4,4]{1,0:T(4,128)} %refs_5_.1), custom_call_target="tpu_custom_call" | custom-call | tf_op jit(solution)/shard_map/pallas_call | solution.py:436
  22.6 1.0 %copy.8 = bf16[1,1,4,128,1024]{4,3,2,1,0:T(8,128)(2,1)} copy(bf16[1,1,4,128,1024]{4,3,2,1,0:T(8,128)(2,1)S(1)} %bitcast.3) | data formatting | bytes 2097152

commit v4 on v3

--- a/solution.py
+++ b/solution.py
@@ -15,7 +15,7 @@
 def fused_kernel(
     nt, nm, nz, g_hbm, gam_hbm, shift_hbm, off_hbm, coup_hbm, nbr_hbm, out_ref,
     g_ref, gam_ref, shift_ref, off_ref, coup_ref, nbr_ref, left, stage, held, fin, parts, tab,
-    load_sem, a_send, a_recv, z_send, z_recv, near_send, near_recv, far_send, far_recv, own_sem,
+    load_sem, a_send, a_recv, z_send, z_recv, near_send, far_send, mixed_recv, own_sem,
 ):
     t, m, z = lax.axis_index("tile"), lax.axis_index("mom"), lax.axis_index("ewin")
     orb, width = g_hbm.shape
@@ -40,7 +40,7 @@
 
     def load(i):
         rows = tile_rows(tile_at(i))
-        return pltpu.make_async_copy(g_hbm.at[rows], g_ref.at[rows], load_sem.at[i])
+        return pltpu.make_async_copy(g_hbm.at[rows], g_ref.at[rows], load_sem.at[i % 2])
 
     def mom_at(j):
         return lax.rem(m + j, nm)
@@ -63,12 +63,15 @@
     def _():
         pl.semaphore_signal(barrier, inc=1, device_id=dev(t, down_mom, z - 1), device_id_type=MESH)
 
-    loads = [pltpu.make_async_copy(gam_hbm, gam_ref, load_sem.at[nt])]
+    loads = [pltpu.make_async_copy(gam_hbm, gam_ref, load_sem.at[2])]
     loads += [load(i) for i in (0, 2, 1, 3)]
     small = ((shift_hbm, shift_ref), (off_hbm, off_ref), (coup_hbm, coup_ref), (nbr_hbm, nbr_ref))
-    small = [pltpu.make_async_copy(src, dst, load_sem.at[nt + 1 + n]) for n, (src, dst) in enumerate(small)]
+    small = [pltpu.make_async_copy(src, dst, load_sem.at[3 + n]) for n, (src, dst) in enumerate(small)]
     for copy in loads + small:
         copy.start()
+
+    def drained(ref, sem):
+        pltpu.make_async_copy(ref, ref, sem).wait()
 
     def times(slot, right):
         both = lax.dot_general(
@@ -116,14 +119,22 @@
     def slot_of(i, j):
         return slots[i] * nm + j
 
+    arrivals = (
+        (0, 4, 1, nm - 1), (0, 1, nm, 2 * nm), (0, 1, 3 * nm, nm),
+        (1, 1, nm, 2 * nm), (1, 1, 3 * nm, nm), (2, 1, nm, 3 * nm), (3, 1, nm, 3 * nm),
+    )
+
+    def awaited(g, i):
+        return 0 if i == 0 else (1, 3, 5, 6)[g] + (1 if i == 2 and g < 2 else 0)
+
     def a_copy(g, i, j):
         v, n = groups[g]
         to = mom_at(j)
         return pltpu.make_async_remote_copy(
             src_ref=stage.at[i, share(to), pl.ds(v, n)],
             dst_ref=held.at[1, pl.ds(v, n), slot_of(i, j)],
-            send_sem=a_send.at[g, i, j],
-            recv_sem=a_recv.at[g, i, j],
+            send_sem=a_send.at[min(i, 1)],
+            recv_sem=a_recv.at[awaited(g, i)],
             device_id=dev(tile_at(i), to, z),
             device_id_type=MESH,
         )
@@ -136,17 +147,16 @@
             if (i, j) != (0, 0):
                 a_copy(g, i, j).start()
 
-    def arrived(g, i):
-        for j in range(nm):
-            if (i, j) != (0, 0):
-                a_copy(g, i, j).wait_recv()
+    def arrived(n):
+        v, units, slot, many = arrivals[n]
+        drained(held.at[1, pl.ds(v, units), pl.ds(slot, many)], a_recv.at[n])
 
     chunks = (
         (0, 1, 0, 1), (1, 3, 0, 1), (0, 4, 1, nm - 1),
         (0, 1, nm, 2 * nm), (0, 1, 3 * nm, nm),
-        (1, 1, nm, 3 * nm), (2, 1, nm, 3 * nm), (3, 1, nm, 3 * nm),
+        (1, 1, nm, 2 * nm), (1, 1, 3 * nm, nm), (2, 1, nm, 3 * nm), (3, 1, nm, 3 * nm),
     )
-    needs = ((0, 2, 3, 4), (1, 5), (6,), (7,))
+    unit_of = (0, 0, 0, 0, 0, 1, 1, 2, 3)
 
     def z_copy(k, up):
         v, n, s, w = chunks[k]
@@ -158,8 +168,8 @@
         return pltpu.make_async_remote_copy(
             src_ref=src,
             dst_ref=dst,
-            send_sem=z_send.at[side, k],
-            recv_sem=z_recv.at[side, k],
+            send_sem=z_send.at[side],
+            recv_sem=z_recv.at[side, unit_of[k]],
             device_id=dev(t, up_mom if up else down_mom, z + 1 if up else z - 1),
             device_id_type=MESH,
         )
@@ -175,20 +185,19 @@
 
     base = lax.rem(ring, 2)
     near, far = lax.rem(base - ring + nt, nt), lax.rem(1 - base - ring + nt, nt)
-    for copy in loads[:3]:
-        copy.wait()
+    loads[0].wait()
+    drained(g_ref.at[pl.ds(0, 2 * tall)], load_sem.at[0])
     scale_rows(near)
     put_cross(base)
-    for copy in loads[3:]:
-        copy.wait()
+    drained(g_ref.at[pl.ds(0, 2 * tall)], load_sem.at[1])
     scale_rows(far)
     put_cross(1 - base)
     pl.semaphore_wait(barrier, nt * nm - 1 + has_up.astype(jnp.int32) + has_down.astype(jnp.int32))
-    send(0, 2)
-    send(0, 0)
     pass_on(0)
     send(0, 1)
     send(0, 3)
+    send(0, 0)
+    send(0, 2)
     scale_rows(lax.rem(near + 2, nt))
     scale_rows(lax.rem(far + 2, nt))
     put_pair(0)
@@ -200,16 +209,11 @@
     put_pair(1)
     send(1, 1)
     put_pair(2)
-    for g, i in ((1, 2), (1, 3), (2, 2), (2, 1), (2, 3), (3, 2), (3, 1), (3, 3)):
+    for g, i in ((1, 3), (1, 2), (2, 2), (2, 1), (2, 3), (3, 2), (3, 1), (3, 3)):
         send(g, i)
-    for g in range(4):
-        arrived(g, 0)
-    pass_on(2)
-    for i in (1, 3):
-        arrived(0, i)
-    pass_on(3)
-    arrived(0, 2)
-    pass_on(4)
+    for n in range(3):
+        arrived(n)
+        pass_on(2 + n)
 
     @pl.when(jnp.logical_not(has_down))
     def _():
@@ -241,9 +245,9 @@
         tab[0, d] = 0.5 * (table[0][d] + table[1][d])
         tab[1, d] = 0.5 * (table[0][d] - table[1][d])
 
-    for i in (1, 3, 2):
-        arrived(1, i)
-    pass_on(5)
+    for n in (3, 4):
+        arrived(n)
+        pass_on(2 + n)
     own_copy().wait()
 
     bases = []
@@ -271,8 +275,8 @@
         return pltpu.make_async_remote_copy(
             src_ref=fin.at[kk, :, pl.ds(lo, n)],
             dst_ref=parts.at[slot, :, pl.ds(row, n)],
-            send_sem=near_send.at[v, h, kk],
-            recv_sem=near_recv.at[v, h, kk],
+            send_sem=near_send,
+            recv_sem=mixed_recv.at[(v + 1) // 2],
             device_id=dev(t, mom_at(kk), z),
             device_id_type=MESH,
         )
@@ -282,8 +286,8 @@
         return pltpu.make_async_remote_copy(
             src_ref=fin.at[kk, :, pl.ds(lo, n)],
             dst_ref=parts.at[slot, :, pl.ds(row, n)],
-            send_sem=far_send.at[v, h, kk],
-            recv_sem=far_recv.at[v, h, kk],
+            send_sem=far_send,
+            recv_sem=mixed_recv.at[(v + 1) // 2],
             device_id=dev(tile_at(step), mom_at(kk), z),
             device_id_type=MESH,
         )
@@ -292,14 +296,12 @@
         return range(2 if v in (1, 2) else 1)
 
     def mix(v):
-        for k in needs[v]:
-            @pl.when(has_down)
+        for side, there in enumerate((has_down, has_up)):
+            @pl.when(there)
             def _():
-                z_copy(k, True).wait_recv()
-
-            @pl.when(has_up)
-            def _():
-                z_copy(k, False).wait_recv()
+                got = held.at[2 * side]
+                got = got.at[pl.ds(0, nm), pl.ds(0, 7)] if v == 0 else got.at[v, pl.ds(nm, 3 * nm)]
+                drained(got, z_recv.at[side, v])
 
         own = pieces(v, m, True)
         weight = [[tab[part, d] for d in range(2 * HW + 1)] for part in range(2)]
@@ -335,14 +337,9 @@
                 if kk > 0:
                     near_copy(v, h, kk, m).start()
 
-    def landed(v):
-        for h in halves(v):
-            for kk in range(nm):
-                who = mom_at(nm - kk)
-                if v < 3:
-                    far_copy(v, h, kk, who, False).wait_recv()
-                if kk > 0:
-                    near_copy(v, h, kk, who).wait_recv()
+    def landed(n):
+        copies, rows = ((2 * nm - 1, qr), (2 * nm - 1, 2 * qr), (nm - 1, qr))[n]
+        drained(parts.at[pl.ds(0, copies), :, pl.ds(0, rows)], mixed_recv.at[n])
 
     def kept(tile):
         found = jnp.float32(0.0)
@@ -376,16 +373,15 @@
             out_ref[e, :, pl.ds(pl.multiple_of(t * tall, tall), tall)] = (re * keep).astype(jnp.bfloat16)
             out_ref[e, :, pl.ds(pl.multiple_of(orb + t * tall, tall), tall)] = (im * keep).astype(jnp.bfloat16)
 
-    for i in (1, 3, 2):
-        arrived(2, i)
-    pass_on(6)
+    arrived(5)
+    pass_on(7)
     mix(0)
-    for i in (1, 3, 2):
-        arrived(3, i)
-    pass_on(7)
-    mix(1)
-    mix(2)
-    mix(3)
+    arrived(6)
+    pass_on(8)
+    drained(stage.at[0, pl.ds(0, nm - 1)], a_send.at[0])
+    drained(stage.at[pl.ds(1, nt - 1)], a_send.at[1])
+    for v in range(1, 4):
+        mix(v)
     landed(0)
 
     @pl.when(ring < 2)
@@ -396,31 +392,18 @@
     def _():
         store(2, tile_at(2), True)
 
+    for side, there in enumerate((has_up, has_down)):
+        @pl.when(there)
+        def _():
+            drained(held.at[1], z_send.at[side])
+
+    drained(fin.at[:, :, pl.ds(0, 3 * qr)], far_send)
     landed(1)
-    landed(2)
     store(0, tile_at(1), False)
     store(1, tile_at(nt - 1), True)
-    landed(3)
+    drained(fin.at[pl.ds(1, nm - 1)], near_send)
+    landed(2)
     store_diagonal()
-
-    for v in range(4):
-        for h in halves(v):
-            for kk in range(nm):
-                if v < 3:
-                    far_copy(v, h, kk, m, True).wait_send()
-                if kk > 0:
-                    near_copy(v, h, kk, m).wait_send()
-    for i, j in pairs[1:]:
-        for g in range(4):
-            a_copy(g, i, j).wait_send()
-    for k in range(len(chunks)):
-        @pl.when(has_up)
-        def _():
-            z_copy(k, True).wait_send()
-
-        @pl.when(has_down)
-        def _():
-            z_copy(k, False).wait_send()
 
 
 def fused(green_ret, injection, mom_shift, phon_off, coupling, tile_nbr):
@@ -448,15 +431,14 @@
             pltpu.VMEM((nm, nt, 4 * qr, 2 * tall), jnp.bfloat16),
             pltpu.VMEM((4, nt, tall, 2 * tall), jnp.bfloat16),
             pltpu.SMEM((nm, 2 * HW + 1), jnp.float32),
-            dma((nt + 5,)),
-            dma((4, nt, nm)),
-            dma((4, nt, nm)),
-            dma((2, 8)),
-            dma((2, 8)),
-            dma((4, 2, nm)),
-            dma((4, 2, nm)),
-            dma((4, 2, nm)),
-            dma((4, 2, nm)),
+            dma((7,)),
+            dma((2,)),
+            dma((7,)),
+            dma((2,)),
+            dma((2, 4)),
+            dma,
+            dma,
+            dma((3,)),
             dma,
         ],
         compiler_params=pltpu.CompilerParams(collective_id=0, has_side_effects=True),

time: 23.7 us -> 21.6 us (0.911)
  Pallas kernels: 22.6 us -> 20.5 us
    pallas_call x1, Pallas kernels: 22.6 us -> 20.5 us  [fused(): pl.pallas_call(lambda *refs: fused_kernel(nt, nm, nz, *refs), out_shape=p...]
where the time goes in v4:
time: 21.6 us; the launch traced here: 21.5 us
  Pallas kernels  20.5 us (95%)
  local copies, waits for them, and re-layouts  0.97 us (4%)
    pallas_call x1, Pallas kernels, fused(): pl.pallas_call(lambda *refs: fused_kernel(nt, nm, nz, *refs), out_shape=p...  20.5 us
    unnamed x1, local copies, waits for them, and re-layouts  0.97 us

profile of v4, /device:TPU:0, one launch (start us, length us, event | category | flops | bytes accessed | tf_op | source)
XLA Modules:
  0.0 21.5 jit_solution(10207339860805909398)
XLA Ops:
  0.0 20.5 %shard_map.64 = bf16[4,128,1024]{2,1,0:T(8,128)(2,1)S(1)} custom-call(bf16[512,1024]{1,0:T(8,128)(2,1)} %bitcast.4, f32[1,512]{1,0:T(1,128)} %bitcast.5, s32[4]{0:T(128)} %refs_2_.1, s32[8]{0:T(128)} %refs_3_.1, f32[4,8]{1,0:T(4,128)} %refs_4_.1, s32[4,4]{1,0:T(4,128)} %refs_5_.1), custom_call_target="tpu_custom_call" | custom-call | tf_op jit(solution)/shard_map/pallas_call | solution.py:419
  20.5 1.0 %copy.8 = bf16[1,1,4,128,1024]{4,3,2,1,0:T(8,128)(2,1)} copy(bf16[1,1,4,128,1024]{4,3,2,1,0:T(8,128)(2,1)S(1)} %bitcast.3) | data formatting | bytes 2097152

commit v5 on v4

--- a/solution.py
+++ b/solution.py
@@ -194,9 +194,9 @@
     put_cross(1 - base)
     pl.semaphore_wait(barrier, nt * nm - 1 + has_up.astype(jnp.int32) + has_down.astype(jnp.int32))
     pass_on(0)
+    send(0, 0)
     send(0, 1)
     send(0, 3)
-    send(0, 0)
     send(0, 2)
     scale_rows(lax.rem(near + 2, nt))
     scale_rows(lax.rem(far + 2, nt))
@@ -375,9 +375,9 @@
 
     arrived(5)
     pass_on(7)
-    mix(0)
     arrived(6)
     pass_on(8)
+    mix(0)
     drained(stage.at[0, pl.ds(0, nm - 1)], a_send.at[0])
     drained(stage.at[pl.ds(1, nt - 1)], a_send.at[1])
     for v in range(1, 4):
@@ -398,12 +398,12 @@
             drained(held.at[1], z_send.at[side])
 
     drained(fin.at[:, :, pl.ds(0, 3 * qr)], far_send)
+    landed(2)
+    store_diagonal()
+    drained(fin.at[pl.ds(1, nm - 1)], near_send)
     landed(1)
     store(0, tile_at(1), False)
     store(1, tile_at(nt - 1), True)
-    drained(fin.at[pl.ds(1, nm - 1)], near_send)
-    landed(2)
-    store_diagonal()
 
 
 def fused(green_ret, injection, mom_shift, phon_off, coupling, tile_nbr):

time: 21.6 us -> 21.5 us (level)
  no operation moved by 1% of the time
where the time goes in v5:
time: 21.5 us; the launch traced here: 21.4 us
  Pallas kernels  20.4 us (95%)
  local copies, waits for them, and re-layouts  0.97 us (5%)
    pallas_call x1, Pallas kernels, fused(): pl.pallas_call(lambda *refs: fused_kernel(nt, nm, nz, *refs), out_shape=p...  20.4 us
    unnamed x1, local copies, waits for them, and re-layouts  0.97 us

profile of v5, /device:TPU:0, one launch (start us, length us, event | category | flops | bytes accessed | tf_op | source)
XLA Modules:
  0.0 21.4 jit_solution(8040149471184917551)
XLA Ops:
  0.0 20.4 %shard_map.64 = bf16[4,128,1024]{2,1,0:T(8,128)(2,1)S(1)} custom-call(bf16[512,1024]{1,0:T(8,128)(2,1)} %bitcast.4, f32[1,512]{1,0:T(1,128)} %bitcast.5, s32[4]{0:T(128)} %refs_2_.1, s32[8]{0:T(128)} %refs_3_.1, f32[4,8]{1,0:T(4,128)} %refs_4_.1, s32[4,4]{1,0:T(4,128)} %refs_5_.1), custom_call_target="tpu_custom_call" | custom-call | tf_op jit(solution)/shard_map/pallas_call | solution.py:419
  20.4 1.0 %copy.8 = bf16[1,1,4,128,1024]{4,3,2,1,0:T(8,128)(2,1)} copy(bf16[1,1,4,128,1024]{4,3,2,1,0:T(8,128)(2,1)S(1)} %bitcast.3) | data formatting | bytes 2097152

commit v6 on v5

--- a/solution.py
+++ b/solution.py
@@ -113,7 +113,7 @@
                 for b in range(2):
                     stage[(i + h) % nt, :, 1 + b, h * hq : (h + 1) * hq, cols] = block[h, :, b]
 
-    groups = ((0, 1), (1, 1), (2, 1), (3, 1))
+    groups = ((0, 1), (1, 1), (2, 1), (3, 1), (1, 3))
     slots = (0, 1, 3, 2)
 
     def slot_of(i, j):
@@ -133,7 +133,7 @@
         return pltpu.make_async_remote_copy(
             src_ref=stage.at[i, share(to), pl.ds(v, n)],
             dst_ref=held.at[1, pl.ds(v, n), slot_of(i, j)],
-            send_sem=a_send.at[min(i, 1)],
+            send_sem=a_send,
             recv_sem=a_recv.at[awaited(g, i)],
             device_id=dev(tile_at(i), to, z),
             device_id_type=MESH,
@@ -202,8 +202,7 @@
     scale_rows(lax.rem(far + 2, nt))
     put_pair(0)
     put_pair(3)
-    for g in (1, 2, 3):
-        send(g, 0)
+    send(4, 0)
     pass_on(1)
     own_copy().start()
     put_pair(1)
@@ -330,12 +329,13 @@
                         if kk > 0 or v < 3:
                             fin[kk, e, rows, cols] = value
 
+        if v < 3:
+            for h in halves(v):
+                for kk in range(nm):
+                    far_copy(v, h, kk, m, True).start()
         for h in halves(v):
-            for kk in range(nm):
-                if v < 3:
-                    far_copy(v, h, kk, m, True).start()
-                if kk > 0:
-                    near_copy(v, h, kk, m).start()
+            for kk in range(1, nm):
+                near_copy(v, h, kk, m).start()
 
     def landed(n):
         copies, rows = ((2 * nm - 1, qr), (2 * nm - 1, 2 * qr), (nm - 1, qr))[n]
@@ -378,8 +378,7 @@
     arrived(6)
     pass_on(8)
     mix(0)
-    drained(stage.at[0, pl.ds(0, nm - 1)], a_send.at[0])
-    drained(stage.at[pl.ds(1, nt - 1)], a_send.at[1])
+    drained(held.at[1, pl.ds(0, 4), pl.ds(0, nt * nm - 1)], a_send)
     for v in range(1, 4):
         mix(v)
     landed(0)
@@ -402,8 +401,8 @@
     store_diagonal()
     drained(fin.at[pl.ds(1, nm - 1)], near_send)
     landed(1)
+    store(1, tile_at(nt - 1), True)
     store(0, tile_at(1), False)
-    store(1, tile_at(nt - 1), True)
 
 
 def fused(green_ret, injection, mom_shift, phon_off, coupling, tile_nbr):
@@ -432,7 +431,7 @@
             pltpu.VMEM((4, nt, tall, 2 * tall), jnp.bfloat16),
             pltpu.SMEM((nm, 2 * HW + 1), jnp.float32),
             dma((7,)),
-            dma((2,)),
+            dma,
             dma((7,)),
             dma((2,)),
             dma((2, 4)),

time: 21.5 us -> 21.5 us (level)
  no operation moved by 1% of the time
where the time goes in v6:
time: 21.5 us; the launch traced here: 21.3 us
  Pallas kernels  20.3 us (94%)
  local copies, waits for them, and re-layouts  0.97 us (5%)
    pallas_call x1, Pallas kernels, fused(): pl.pallas_call(lambda *refs: fused_kernel(nt, nm, nz, *refs), out_shape=p...  20.3 us
    unnamed x1, local copies, waits for them, and re-layouts  0.97 us

profile of v6, /device:TPU:0, one launch (start us, length us, event | category | flops | bytes accessed | tf_op | source)
XLA Modules:
  0.0 21.3 jit_solution(6182026003780335322)
XLA Ops:
  0.0 20.3 %shard_map.64 = bf16[4,128,1024]{2,1,0:T(8,128)(2,1)S(1)} custom-call(bf16[512,1024]{1,0:T(8,128)(2,1)} %bitcast.4, f32[1,512]{1,0:T(1,128)} %bitcast.5, s32[4]{0:T(128)} %refs_2_.1, s32[8]{0:T(128)} %refs_3_.1, f32[4,8]{1,0:T(4,128)} %refs_4_.1, s32[4,4]{1,0:T(4,128)} %refs_5_.1), custom_call_target="tpu_custom_call" | custom-call | tf_op jit(solution)/shard_map/pallas_call | solution.py:418
  20.3 1.0 %copy.8 = bf16[1,1,4,128,1024]{4,3,2,1,0:T(8,128)(2,1)} copy(bf16[1,1,4,128,1024]{4,3,2,1,0:T(8,128)(2,1)S(1)} %bitcast.3) | data formatting | bytes 2097152

commit v7 on v6

--- a/solution.py
+++ b/solution.py
@@ -152,11 +152,11 @@
         drained(held.at[1, pl.ds(v, units), pl.ds(slot, many)], a_recv.at[n])
 
     chunks = (
-        (0, 1, 0, 1), (1, 3, 0, 1), (0, 4, 1, nm - 1),
+        (0, 1, 0, 1), (1, 3, 0, 1), (0, 3, 1, nm - 1),
         (0, 1, nm, 2 * nm), (0, 1, 3 * nm, nm),
-        (1, 1, nm, 2 * nm), (1, 1, 3 * nm, nm), (2, 1, nm, 3 * nm), (3, 1, nm, 3 * nm),
+        (1, 1, nm, 2 * nm), (1, 1, 3 * nm, nm), (2, 1, nm, 3 * nm), (3, 1, 1, 4 * nm - 1),
     )
-    unit_of = (0, 0, 0, 0, 0, 1, 1, 2, 3)
+    unit_of = (0, 4, 4, 0, 0, 1, 1, 2, 3)
 
     def z_copy(k, up):
         v, n, s, w = chunks[k]
@@ -299,7 +299,10 @@
             @pl.when(there)
             def _():
                 got = held.at[2 * side]
-                got = got.at[pl.ds(0, nm), pl.ds(0, 7)] if v == 0 else got.at[v, pl.ds(nm, 3 * nm)]
+                if v == 0:
+                    drained(got.at[pl.ds(1, 3), pl.ds(0, nm)], z_recv.at[side, 4])
+                first = (nm - 1 if v == 0 else nm, nm, nm, 1)[v]
+                got = got.at[v, pl.ds(first, (3 * nm + 1, 3 * nm, 3 * nm, 4 * nm - 1)[v])]
                 drained(got, z_recv.at[side, v])
 
         own = pieces(v, m, True)
@@ -434,7 +437,7 @@
             dma,
             dma((7,)),
             dma((2,)),
-            dma((2, 4)),
+            dma((2, 5)),
             dma,
             dma,
             dma((3,)),

time: 21.5 us -> 21.5 us (level)
  no operation moved by 1% of the time
where the time goes in v7:
time: 21.5 us; the launch traced here: 21.3 us
  Pallas kernels  20.4 us (95%)
  local copies, waits for them, and re-layouts  0.97 us (5%)
    pallas_call x1, Pallas kernels, fused(): pl.pallas_call(lambda *refs: fused_kernel(nt, nm, nz, *refs), out_shape=p...  20.4 us
    unnamed x1, local copies, waits for them, and re-layouts  0.97 us

profile of v7, /device:TPU:0, one launch (start us, length us, event | category | flops | bytes accessed | tf_op | source)
XLA Modules:
  0.0 21.3 jit_solution(16547448118789669650)
XLA Ops:
  0.0 20.4 %shard_map.64 = bf16[4,128,1024]{2,1,0:T(8,128)(2,1)S(1)} custom-call(bf16[512,1024]{1,0:T(8,128)(2,1)} %bitcast.4, f32[1,512]{1,0:T(1,128)} %bitcast.5, s32[4]{0:T(128)} %refs_2_.1, s32[8]{0:T(128)} %refs_3_.1, f32[4,8]{1,0:T(4,128)} %refs_4_.1, s32[4,4]{1,0:T(4,128)} %refs_5_.1), custom_call_target="tpu_custom_call" | custom-call | tf_op jit(solution)/shard_map/pallas_call | solution.py:421
  20.4 1.0 %copy.8 = bf16[1,1,4,128,1024]{4,3,2,1,0:T(8,128)(2,1)} copy(bf16[1,1,4,128,1024]{4,3,2,1,0:T(8,128)(2,1)S(1)} %bitcast.3) | data formatting | bytes 2097152
